TPU v7x, 32 devices: a whole 2x2x4 slice. The times are simulated.
32 devices in a mesh: dp: 2 (over core), expert: 16 (over z, y, x).
Axes of the slice: x: 2, y: 2, z: 4, core: 2. Of those that a mesh axis runs over, the one named last changes fastest.
Arguments:
- tokens: bfloat16 [2048, 2048], P('expert'), may hold values from -6 to 6
- out_grad: bfloat16 [2048, 2048], P('expert'), may hold values from -6 to 6
- route_ids: int32 [2048, 8], P('expert'), may hold values from 0 to 15, all different within a row; in each aligned block of 128 rows (0 to 127, 128 to 255, ...) at most 72 rows name the same one
- route_probs: float32 [2048, 8], P('expert'), may hold values from 0.05 to 1
- gate_store: bfloat16 [16, 2048, 768], P(None, 'expert', 'dp'), may hold values from -0.125 to 0.125
- up_store: bfloat16 [16, 2048, 768], P(None, 'expert', 'dp'), may hold values from -0.125 to 0.125
- down_store: bfloat16 [16, 2048, 768], P(None, 'expert', 'dp'), may hold values from -0.21875 to 0.21875
Outputs:
- grad_gate: bfloat16 [16, 2048, 768], P('expert', None, 'dp')
- grad_up: bfloat16 [16, 2048, 768], P('expert', None, 'dp')
- grad_down: bfloat16 [16, 2048, 768], P('expert', None, 'dp')
- grad_tokens: bfloat16 [2048, 2048], P('expert')
Inputs may be any that keep to these rules, and one draw needn't show every extreme that they name: `route_ids`: among the 128 tokens of one device no expert is named more than 72 times, and in every draw some expert is named exactly 72 times by some device's tokens.
All inputs are finite; a program needn't handle non-finite values.
Results may differ from a plain program's by a relative error of at most 0.0065.
Values may be sent and summed in bfloat16 or wider, within the bound.
A program may use at most 128 MiB of HBM per device.

v0:
```python
import jax
import jax.numpy as jnp
from jax import lax
from jax.sharding import PartitionSpec as P


def joined(own, other):
    first = lax.axis_index("dp") == 0
    return jnp.where(first, jnp.concatenate([own, other], -1), jnp.concatenate([other, own], -1))


def swapped(part):
    return lax.ppermute(part, "dp", [(0, 1), (1, 0)])


def placed(tokens, out_grad, route_ids, route_probs, gate_store, up_store, down_store):
    tok_rows, model_width = tokens.shape
    top_count = route_ids.shape[1]
    experts = lax.axis_size("expert")
    capacity = max(2, 9 * tok_rows * top_count // (8 * experts))
    slots = experts * capacity
    width = model_width // 2
    here = lax.axis_index("dp") * width
    there = width - here
    f32, bf16 = (jnp.float32, jnp.bfloat16)
    chosen = route_ids[:, :, None] == jnp.arange(experts, dtype=jnp.int32)[None, None, :]
    weight = jnp.sum(jnp.where(chosen, route_probs[:, :, None], 0.0), axis=1)
    named = jnp.any(chosen, axis=1)
    earlier = jnp.arange(tok_rows)[:, None] > jnp.arange(tok_rows)[None, :]
    rank = jnp.dot(earlier.astype(bf16), named.astype(bf16), preferred_element_type=f32)
    rank = jnp.where(named, rank, -1.0)
    hit = rank.T[:, None, :] == jnp.arange(capacity, dtype=f32)[None, :, None]
    slot_prob = jnp.sum(jnp.where(hit, weight.T[:, None, :], 0.0), axis=2)
    place = hit.astype(bf16).reshape(slots, tok_rows)
    x_part = jnp.dot(
        place, lax.dynamic_slice_in_dim(tokens, here, width, 1), preferred_element_type=f32
    ).astype(bf16)
    dy_part = (
        jnp.dot(
            place, lax.dynamic_slice_in_dim(out_grad, here, width, 1), preferred_element_type=f32
        )
        * slot_prob.reshape(slots, 1)
    ).astype(bf16)

    def exchange(a):
        return lax.all_to_all(a, "expert", split_axis=0, concat_axis=0, tiled=True)

    def panel(store):
        return lax.all_to_all(store, "expert", split_axis=0, concat_axis=1, tiled=True)[0]

    x_own = exchange(x_part.reshape(experts, capacity, width)).reshape(slots, width)
    gate_panel = panel(gate_store)
    up_panel = panel(up_store)
    dy_own = exchange(dy_part.reshape(experts, capacity, width)).reshape(slots, width)
    down_panel = panel(down_store)
    rows_in = joined(x_own, swapped(x_own))
    dy_rows = joined(dy_own, swapped(dy_own))
    gate_pre = jnp.dot(rows_in, gate_panel, preferred_element_type=f32)
    up_pre = jnp.dot(rows_in, up_panel, preferred_element_type=f32)
    sig = jax.nn.sigmoid(gate_pre)
    activation = (gate_pre * sig * up_pre).astype(bf16)
    act_grad = jnp.dot(dy_rows, down_panel, preferred_element_type=f32)
    up_grad = (act_grad * gate_pre * sig).astype(bf16)
    gate_grad = (act_grad * up_pre * sig * (1.0 + gate_pre * (1.0 - sig))).astype(bf16)
    back = (((1,), (1,)), ((), ()))

    def slot_part(start):
        rows = [lax.dynamic_slice_in_dim(w, start, width, 0) for w in (gate_panel, up_panel)]
        return lax.dot_general(
            gate_grad, rows[0], back, preferred_element_type=f32
        ) + lax.dot_general(up_grad, rows[1], back, preferred_element_type=f32)

    arrived = swapped(slot_part(there).astype(bf16))
    summed = (slot_part(here) + arrived.astype(f32)).astype(bf16)
    returned = exchange(summed.reshape(experts, capacity, width)).reshape(slots, width)
    share = lax.dot_general(
        place, returned, (((0,), (0,)), ((), ())), preferred_element_type=f32
    ).astype(bf16)
    grad_tokens = joined(share, swapped(share))
    outer = (((0,), (0,)), ((), ()))
    grad_down = lax.dot_general(dy_rows, activation, outer, preferred_element_type=f32).astype(bf16)
    grad_gate = lax.dot_general(rows_in, gate_grad, outer, preferred_element_type=f32).astype(bf16)
    grad_up = lax.dot_general(rows_in, up_grad, outer, preferred_element_type=f32).astype(bf16)
    return (grad_gate[None], grad_up[None], grad_down[None], grad_tokens)


def solution(mesh):
    return jax.shard_map(
        placed,
        mesh=mesh,
        in_specs=(
            P("expert", None),
            P("expert", None),
            P("expert", None),
            P("expert", None),
            P(None, "expert", "dp"),
            P(None, "expert", "dp"),
            P(None, "expert", "dp"),
        ),
        out_specs=(
            P("expert", None, "dp"),
            P("expert", None, "dp"),
            P("expert", None, "dp"),
            P("expert", None),
        ),
        check_vma=False,
    )
```

profile of v0, /device:TPU:15, one launch (start us, length us, event | category | flops | bytes accessed | tf_op | source)
XLA Modules:
  0.0 329.0 jit_solution(13981634180581247777)
XLA Ops:
  0.6 0.0 copy-start
  0.6 41.9 %all_to_all.42 = bf16[16,128,384]{2,1,0:T(8,128)(2,1)} all-to-all(bf16[16,128,384]{2,1,0:T(8,128)(2,1)} %param.11), channel_id=1, replica_groups=mesh['dp'=2,'expert'=16] {'expert'}, dimensions={0} | all-to-all | bytes 3145728 | tf_op jit(solution)/shard_map/all_to_all | solution.py:49
  42.5 5.9 %all-to-all-start.3 = ((bf16[16,128,384]{2,1,0:T(8,128)(2,1)}), bf16[16,128,384]{2,1,0:T(8,128)(2,1)S(1)}, u32[]{:S(2)}, u32[]{:S(2)}) async-start(bf16[16,128,384]{2,1,0:T(8,128)(2,1)} %param.12), calls=%async_computation.3 | async-start | bytes 3145728 | tf_op jit(solution)/shard_map/all_to_all | solution.py:49
  48.4 0.1 eq.49
  48.5 0.0 copy-done.6
  48.5 0.1 convolution_select_fusion
  48.7 0.2 bitcast_compare_fusion
  48.9 0.0 copy-done
  48.9 2.2 convolution_convert_fusion
  51.1 33.7 %all-to-all-done.3 = bf16[16,128,384]{2,1,0:T(8,128)(2,1)S(1)} async-done(((bf16[16,128,384]{2,1,0:T(8,128)(2,1)}), bf16[16,128,384]{2,1,0:T(8,128)(2,1)S(1)}, u32[]{:S(2)}, u32[]{:S(2)}) %all-to-all-start.3) | async-done | bytes 1572896 | tf_op jit(solution)/shard_map/all_to_all | solution.py:49
  84.8 4.7 %all-to-all-start = ((bf16[16,72,1024]{2,1,0:T(8,128)(2,1)}), bf16[16,72,1024]{2,1,0:T(8,128)(2,1)}, u32[]{:S(2)}, u32[]{:S(2)}) async-start(bf16[16,72,1024]{2,1,0:T(8,128)(2,1)} %bitcast.2), calls=%async_computation | async-start | bytes 4718592 | tf_op jit(solution)/shard_map/all_to_all | solution.py:46
  89.5 0.0 copy-done.7
  89.5 0.3 select_reduce_fusion
  89.9 0.1 mul.38
  90.0 0.0 copy-done.5
  90.0 2.2 fusion
  92.2 50.3 %all-to-all-done = bf16[16,72,1024]{2,1,0:T(8,128)(2,1)} async-done(((bf16[16,72,1024]{2,1,0:T(8,128)(2,1)}), bf16[16,72,1024]{2,1,0:T(8,128)(2,1)}, u32[]{:S(2)}, u32[]{:S(2)}) %all-to-all-start) | async-done | bytes 2359328 | tf_op jit(solution)/shard_map/all_to_all | solution.py:46
  142.5 4.6 %all-to-all-start.1 = ((bf16[16,72,1024]{2,1,0:T(8,128)(2,1)}), bf16[16,72,1024]{2,1,0:T(8,128)(2,1)}, u32[]{:S(2)}, u32[]{:S(2)}) async-start(bf16[16,72,1024]{2,1,0:T(8,128)(2,1)} %bitcast.5), calls=%async_computation.1 | async-start | bytes 4718592 | tf_op jit(solution)/shard_map/all_to_all | solution.py:46
  147.1 2.2 collective-permute-start
  149.2 50.9 %all-to-all-done.1 = bf16[16,72,1024]{2,1,0:T(8,128)(2,1)} async-done(((bf16[16,72,1024]{2,1,0:T(8,128)(2,1)}), bf16[16,72,1024]{2,1,0:T(8,128)(2,1)}, u32[]{:S(2)}, u32[]{:S(2)}) %all-to-all-start.1) | async-done | bytes 2359328 | tf_op jit(solution)/shard_map/all_to_all | solution.py:46
  200.1 4.6 %all-to-all-start.2 = ((bf16[16,128,384]{2,1,0:T(8,128)(2,1)}), bf16[16,128,384]{2,1,0:T(8,128)(2,1)}, u32[]{:S(2)}, u32[]{:S(2)}) async-start(bf16[16,128,384]{2,1,0:T(8,128)(2,1)} %param.13), calls=%async_computation.2 | async-start | bytes 3145728 | tf_op jit(solution)/shard_map/all_to_all | solution.py:49
  204.7 2.2 collective-permute-start.1
  206.9 0.0 collective-permute-done
  206.9 8.1 %fusion.29 = f32[1152,384]{1,0:T(8,128)} fusion(bf16[2048,384]{1,0:T(8,128)(2,1)} %bitcast.40, bf16[1152,1024]{1,0:T(8,128)(2,1)} %collective-permute-done, bf16[1152,1024]{1,0:T(8,128)(2,1)} %bitcast.3, pred[]{:T(512)S(6)} %eq.42), kind=kOutput, calls=%fused_computation.50 | convolution fusion | flops 1833172992 | bytes 8060929 | tf_op jit(solution)/shard_map/dot_general | solution.py:58
  215.0 7.6 %fusion.30 = f32[1152,384]{1,0:T(8,128)} fusion(bf16[2048,384]{1,0:T(8,128)(2,1)S(1)} %bitcast.37, bf16[1152,1024]{1,0:T(8,128)(2,1)} %collective-permute-done, bf16[1152,1024]{1,0:T(8,128)(2,1)} %bitcast.3, pred[]{:T(512)S(6)} %eq.42), kind=kOutput, calls=%fused_computation.51 | convolution fusion | flops 1833172992 | bytes 8060929 | tf_op jit(solution)/shard_map/dot_general | solution.py:59
  222.5 18.1 %all-to-all-done.2 = bf16[16,128,384]{2,1,0:T(8,128)(2,1)} async-done(((bf16[16,128,384]{2,1,0:T(8,128)(2,1)}), bf16[16,128,384]{2,1,0:T(8,128)(2,1)}, u32[]{:S(2)}, u32[]{:S(2)}) %all-to-all-start.2) | async-done | bytes 1572896 | tf_op jit(solution)/shard_map/all_to_all | solution.py:49
  240.7 0.0 collective-permute-done.1
  240.7 7.5 %multiply_convert_fusion.1 = (bf16[1152,384]{1,0:T(8,128)(2,1)S(1)}, bf16[1152,384]{1,0:T(8,128)(2,1)S(1)}) fusion(f32[1152,384]{1,0:T(8,128)} %fusion.29, f32[1152,384]{1,0:T(8,128)} %fusion.30, bf16[2048,384]{1,0:T(8,128)(2,1)} %bitcast.7, bf16[1152,1024]{1,0:T(8,128)(2,1)} %collective-permute-done.1, bf16[1152,1024]{1,0:T(8,128)(2,1)} %bitcast.6, ...), kind=kOutput, calls=%fused_computation.16 | convolution fusion | flops 1838923776 | bytes 11599873 | tf_op jit(solution)/shard_map/dot_general | solution.py:62
  248.2 0.0 copy-start.1
  248.2 0.0 copy-start.4
  248.2 0.0 copy-done.3
  248.2 1.4 fusion.9
  249.7 1.5 fusion.1
  251.1 1.5 collective-permute-start.2
  252.6 0.0 copy-done.1
  252.6 1.4 fusion.14
  254.0 2.7 collective-permute-done.2
  256.7 2.9 add_convert_fusion
  259.7 5.0 %all-to-all-start.5 = ((bf16[16,72,1024]{2,1,0:T(8,128)(2,1)}), bf16[16,72,1024]{2,1,0:T(8,128)(2,1)S(1)}, u32[]{:S(2)}, u32[]{:S(2)}) async-start(bf16[16,72,1024]{2,1,0:T(8,128)(2,1)} %bitcast.36), calls=%async_computation.5 | async-start | bytes 4718592 | tf_op jit(solution)/shard_map/all_to_all | solution.py:46
  264.7 0.0 copy-start.9
  264.7 8.1 %fusion.3 = bf16[1,2048,384]{2,1,0:T(8,128)(2,1)} fusion(bf16[1152,384]{1,0:T(8,128)(2,1)} %copy-done.4, bf16[1152,1024]{1,0:T(8,128)(2,1)} %collective-permute-done, bf16[1152,1024]{1,0:T(8,128)(2,1)} %bitcast.3, pred[]{:T(512)S(6)} %eq.42), kind=kOutput, calls=%fused_computation.13 | convolution fusion | flops 1833959424 | bytes 7176193 | tf_op jit(solution)/shard_map/dot_general | solution.py:83
  272.8 8.1 %fusion.4 = bf16[1,2048,384]{2,1,0:T(8,128)(2,1)} fusion(f32[1152,384]{1,0:T(8,128)S(1)} %copy-done.9, f32[1152,384]{1,0:T(8,128)S(1)} %copy-done.8, bf16[1152,1024]{1,0:T(8,128)(2,1)} %collective-permute-done.1, bf16[1152,1024]{1,0:T(8,128)(2,1)} %bitcast.6, pred[]{:T(512)S(6)} %eq.42), kind=kOutput, calls=%fused_computation.14 | convolution fusion | flops 1836613632 | bytes 9830401 | tf_op jit(solution)/shard_map/dot_general | solution.py:81
  280.9 37.3 %all-to-all-done.5 = bf16[16,72,1024]{2,1,0:T(8,128)(2,1)S(1)} async-done(((bf16[16,72,1024]{2,1,0:T(8,128)(2,1)}), bf16[16,72,1024]{2,1,0:T(8,128)(2,1)S(1)}, u32[]{:S(2)}, u32[]{:S(2)}) %all-to-all-start.5) | async-done | bytes 2359328 | tf_op jit(solution)/shard_map/all_to_all | solution.py:46
  318.2 0.6 fusion.5
  318.8 1.5 collective-permute-start.3
  320.2 7.8 %fusion.2 = bf16[1,2048,384]{2,1,0:T(8,128)(2,1)} fusion(bf16[1152,384]{1,0:T(8,128)(2,1)S(1)} %copy-done.2, bf16[1152,1024]{1,0:T(8,128)(2,1)} %collective-permute-done, bf16[1152,1024]{1,0:T(8,128)(2,1)} %bitcast.3, pred[]{:T(512)S(6)} %eq.42), kind=kOutput, calls=%fused_computation.12 | convolution fusion | flops 1833959424 | bytes 7176193 | tf_op jit(solution)/shard_map/dot_general | solution.py:82
  328.1 0.0 collective-permute-done.3
  328.1 0.9 maximum_select_fusion.4
  (13 shorter events, 0.1 us)
Async XLA Ops:
  0.6 48.3 %copy-start = (bf16[128,2048]{1,0:T(8,128)(2,1)S(1)}, bf16[128,2048]{1,0:T(8,128)(2,1)}, u32[]{:S(2)}) copy-start(bf16[128,2048]{1,0:T(8,128)(2,1)} %param.7) | copy-start | bytes 1572868
  42.5 6.0 %copy-start.6 = (s32[128,8]{0,1:T(8,128)S(1)}, s32[128,8]{0,1:T(8,128)}, u32[]{:S(2)}) copy-start(s32[128,8]{0,1:T(8,128)} %param.9) | copy-start | bytes 12292
  42.5 42.3 %all-to-all-start.3 = ((bf16[16,128,384]{2,1,0:T(8,128)(2,1)}), bf16[16,128,384]{2,1,0:T(8,128)(2,1)S(1)}, u32[]{:S(2)}, u32[]{:S(2)}) async-start(bf16[16,128,384]{2,1,0:T(8,128)(2,1)} %param.12), calls=%async_computation.3 | async-start | bytes 3145728 | tf_op jit(solution)/shard_map/all_to_all | solution.py:49
  84.8 4.7 %copy-start.7 = (f32[128,8]{0,1:T(8,128)S(1)}, f32[128,8]{0,1:T(8,128)}, u32[]{:S(2)}) copy-start(f32[128,8]{0,1:T(8,128)} %param.10) | copy-start | bytes 12292
  84.8 5.2 %copy-start.5 = (bf16[128,2048]{1,0:T(8,128)(2,1)S(1)}, bf16[128,2048]{1,0:T(8,128)(2,1)}, u32[]{:S(2)}) copy-start(bf16[128,2048]{1,0:T(8,128)(2,1)} %param.8) | copy-start | bytes 1572868
  84.8 57.7 %all-to-all-start = ((bf16[16,72,1024]{2,1,0:T(8,128)(2,1)}), bf16[16,72,1024]{2,1,0:T(8,128)(2,1)}, u32[]{:S(2)}, u32[]{:S(2)}) async-start(bf16[16,72,1024]{2,1,0:T(8,128)(2,1)} %bitcast.2), calls=%async_computation | async-start | bytes 4718592 | tf_op jit(solution)/shard_map/all_to_all | solution.py:46
  142.5 57.6 %all-to-all-start.1 = ((bf16[16,72,1024]{2,1,0:T(8,128)(2,1)}), bf16[16,72,1024]{2,1,0:T(8,128)(2,1)}, u32[]{:S(2)}, u32[]{:S(2)}) async-start(bf16[16,72,1024]{2,1,0:T(8,128)(2,1)} %bitcast.5), calls=%async_computation.1 | async-start | bytes 4718592 | tf_op jit(solution)/shard_map/all_to_all | solution.py:46
  147.1 59.8 %collective-permute-start = (bf16[1152,1024]{1,0:T(8,128)(2,1)}, bf16[1152,1024]{1,0:T(8,128)(2,1)}, u32[]{:S(2)}, u32[]{:S(2)}) collective-permute-start(bf16[1152,1024]{1,0:T(8,128)(2,1)} %bitcast.3), channel_id=1, source_target_pairs={{0,16},{16,0},{1,17},{17,1},{2,18},{18,2},{3,19},{19,3},{4,20},{20... | collective-permute-start | bytes 7077896 | tf_op jit(solution)/shard_map/ppermute | solution.py:13
  200.1 40.5 %all-to-all-start.2 = ((bf16[16,128,384]{2,1,0:T(8,128)(2,1)}), bf16[16,128,384]{2,1,0:T(8,128)(2,1)}, u32[]{:S(2)}, u32[]{:S(2)}) async-start(bf16[16,128,384]{2,1,0:T(8,128)(2,1)} %param.13), calls=%async_computation.2 | async-start | bytes 3145728 | tf_op jit(solution)/shard_map/all_to_all | solution.py:49
  204.7 36.0 %collective-permute-start.1 = (bf16[1152,1024]{1,0:T(8,128)(2,1)}, bf16[1152,1024]{1,0:T(8,128)(2,1)}, u32[]{:S(2)}, u32[]{:S(2)}) collective-permute-start(bf16[1152,1024]{1,0:T(8,128)(2,1)} %bitcast.6), channel_id=1, source_target_pairs={{0,16},{16,0},{1,17},{17,1},{2,18},{18,2},{3,19},{19,3},{4,20},{20... | collective-permute-start | bytes 7077896 | tf_op jit(solution)/shard_map/ppermute | solution.py:13
  240.7 7.5 %copy-start.3 = (bf16[16,128,384]{2,1,0:T(8,128)(2,1)S(1)}, bf16[16,128,384]{2,1,0:T(8,128)(2,1)}, u32[]{:S(2)}) copy-start(bf16[16,128,384]{2,1,0:T(8,128)(2,1)} %all_to_all.42) | copy-start | bytes 4718596
  248.2 4.4 %copy-start.1 = (bf16[1152,384]{1,0:T(8,128)(2,1)}, bf16[1152,384]{1,0:T(8,128)(2,1)S(1)}, u32[]{:S(2)}) copy-start(bf16[1152,384]{1,0:T(8,128)(2,1)S(1)} %get-tuple-element.5) | copy-start | bytes 2654212
  248.2 8.5 %copy-start.4 = (bf16[1152,384]{1,0:T(8,128)(2,1)}, bf16[1152,384]{1,0:T(8,128)(2,1)S(1)}, u32[]{:S(2)}) copy-start(bf16[1152,384]{1,0:T(8,128)(2,1)S(1)} %get-tuple-element.4) | copy-start | bytes 2654212
  251.1 5.6 %collective-permute-start.2 = (bf16[1152,1024]{1,0:T(8,128)(2,1)S(1)}, bf16[1152,1024]{1,0:T(8,128)(2,1)S(1)}, u32[]{:S(2)}, u32[]{:S(2)}) collective-permute-start(bf16[1152,1024]{1,0:T(8,128)(2,1)S(1)} %fusion.1), channel_id=1, source_target_pairs={{0,16},{16,0},{1,17},{17,1},{2,18},{18,2},{3,19},{19,3},{4,20},{20... | collective-permute-start | bytes 7077896 | tf_op jit(solution)/shard_map/ppermute | solution.py:13
  259.7 58.5 %all-to-all-start.5 = ((bf16[16,72,1024]{2,1,0:T(8,128)(2,1)}), bf16[16,72,1024]{2,1,0:T(8,128)(2,1)S(1)}, u32[]{:S(2)}, u32[]{:S(2)}) async-start(bf16[16,72,1024]{2,1,0:T(8,128)(2,1)} %bitcast.36), calls=%async_computation.5 | async-start | bytes 4718592 | tf_op jit(solution)/shard_map/all_to_all | solution.py:46
  264.7 8.2 %copy-start.8 = (f32[1152,384]{1,0:T(8,128)S(1)}, f32[1152,384]{1,0:T(8,128)}, u32[]{:S(2)}) copy-start(f32[1152,384]{1,0:T(8,128)} %fusion.29) | copy-start | bytes 5308420
  264.7 8.2 %copy-start.9 = (f32[1152,384]{1,0:T(8,128)S(1)}, f32[1152,384]{1,0:T(8,128)}, u32[]{:S(2)}) copy-start(f32[1152,384]{1,0:T(8,128)} %fusion.30) | copy-start | bytes 5308420
  318.2 2.0 copy-start.2
  318.8 9.3 %collective-permute-start.3 = (bf16[128,1024]{1,0:T(8,128)(2,1)S(1)}, bf16[128,1024]{1,0:T(8,128)(2,1)S(1)}, u32[]{:S(2)}, u32[]{:S(2)}) collective-permute-start(bf16[128,1024]{1,0:T(8,128)(2,1)S(1)} %fusion.5), channel_id=1, source_target_pairs={{0,16},{16,0},{1,17},{17,1},{2,18},{18,2},{3,19},{19,3},{4,20},{20... | collective-permute-start | bytes 786440 | tf_op jit(solution)/shard_map/ppermute | solution.py:13
where the time goes:
time: 330 us; the launch traced here: 329 us
  waiting for transfers between devices  193 us (58%)
  matrix products  59.6 us (18%)
  blocking collectives  41.9 us (13%)
  starting transfers between devices  32 us (10%)
    all_to_all x3, waiting for transfers between devices, exchange(): return lax.all_to_all(a, 'expert', split_axis=0, concat_axis=0, tiled=True)  138 us
    all_to_all x2, waiting for transfers between devices, panel(): lax.all_to_all(store, 'expert', split_axis=0, concat_axis=1, tiled=True)[0]  51.8 us
    all_to_all x1, blocking collectives, panel(): lax.all_to_all(store, 'expert', split_axis=0, concat_axis=1, tiled=True)[0]  41.9 us
    all_to_all x3, starting transfers between devices, exchange(): return lax.all_to_all(a, 'expert', split_axis=0, concat_axis=0, tiled=True)  14.3 us
    all_to_all x2, starting transfers between devices, panel(): lax.all_to_all(store, 'expert', split_axis=0, concat_axis=1, tiled=True)[0]  10.4 us
    dot_general x1, matrix products, placed(): lax.dot_general(rows_in, up_grad, outer, preferred_element_type=f32)  8.14 us
    dot_general x1, matrix products, placed(): gate_pre = jnp.dot(rows_in, gate_panel, preferred_element_type=f32)  8.1 us
    dot_general x1, matrix products, placed(): lax.dot_general(dy_rows, activation, outer, preferred_element_type=f32)  8.06 us
  transfers between devices with their start and end apart: 9, of which 6 were waited for; matrix products, arithmetic and copies ran while one was open for 14% of the time, Pallas kernels for 0%

commit v1 on v0

--- a/solution.py
+++ b/solution.py
@@ -46,7 +46,12 @@
         return lax.all_to_all(a, "expert", split_axis=0, concat_axis=0, tiled=True)
 
     def panel(store):
-        return lax.all_to_all(store, "expert", split_axis=0, concat_axis=1, tiled=True)[0]
+        return jnp.concatenate(
+            lax.all_to_all(
+                jnp.stack(jnp.split(store, lax.axis_size("expert"), axis=0)), "expert", 0, 0
+            ),
+            axis=1,
+        )[0]
 
     x_own = exchange(x_part.reshape(experts, capacity, width)).reshape(slots, width)
     gate_panel = panel(gate_store)

time: 330 us -> 358 us (1.085)
  local copies, waits for them, and re-layouts: 0.23 us -> 74.3 us
  blocking collectives: 41.9 us -> 0 us
  waiting for transfers between devices: 193 us -> 180 us
  starting transfers between devices: 32 us -> 37.4 us
    unnamed x20 -> x63, local copies, waits for them, and re-layouts: 0.05 us -> 69.5 us
    all_to_all x1 -> x0, blocking collectives: 41.9 us -> none  [panel(): lax.all_to_all(store, 'expert', split_axis=0, concat_axis=1, tiled=True)[0]]
    all_to_all x3, waiting for transfers between devices: 138 us -> 113 us  [exchange(): return lax.all_to_all(a, 'expert', split_axis=0, concat_axis=0, tiled=True)]
    all_to_all x2 -> x3, waiting for transfers between devices: 51.8 us -> 63.7 us  [panel(): lax.all_to_all(jnp.stack(jnp.split(store, lax.axis_size('expert'), axis=0...]
    all_to_all x2 -> x3, starting transfers between devices: 10.4 us -> 15.7 us  [panel(): lax.all_to_all(jnp.stack(jnp.split(store, lax.axis_size('expert'), axis=0...]
    another operation x0 -> x3, local copies, waits for them, and re-layouts: none -> 4.63 us  [panel(): jnp.stack(jnp.split(store, lax.axis_size('expert'), axis=0))]
  transfers between devices with their start and end apart: 9 -> 10, of which waited for: 6 -> 7; matrix products, arithmetic and copies ran while one was open for 14% -> 27% of each run, Pallas kernels for 0% -> 0%
where the time goes in v1:
time: 358 us; the launch traced here: 356 us
  waiting for transfers between devices  180 us (50%)
  local copies, waits for them, and re-layouts  74.3 us (21%)
  matrix products  61.8 us (17%)
  starting transfers between devices  37.4 us (10%)
    all_to_all x3, waiting for transfers between devices, exchange(): return lax.all_to_all(a, 'expert', split_axis=0, concat_axis=0, tiled=True)  113 us
    unnamed x63, local copies, waits for them, and re-layouts  69.5 us
    all_to_all x3, waiting for transfers between devices, panel(): lax.all_to_all(jnp.stack(jnp.split(store, lax.axis_size('expert'), axis=0...  63.7 us
    all_to_all x3, starting transfers between devices, panel(): lax.all_to_all(jnp.stack(jnp.split(store, lax.axis_size('expert'), axis=0...  15.7 us
    all_to_all x3, starting transfers between devices, exchange(): return lax.all_to_all(a, 'expert', split_axis=0, concat_axis=0, tiled=True)  14.4 us
    dot_general x1, matrix products, placed(): lax.dot_general(rows_in, up_grad, outer, preferred_element_type=f32)  8.14 us
    dot_general x1, matrix products, placed(): lax.dot_general(dy_rows, activation, outer, preferred_element_type=f32)  8.06 us
    dot_general x1, matrix products, placed(): up_pre = jnp.dot(rows_in, up_panel, preferred_element_type=f32)  8 us
  transfers between devices with their start and end apart: 10, of which 7 were waited for; matrix products, arithmetic and copies ran while one was open for 27% of the time, Pallas kernels for 0%

profile of v1, /device:TPU:15, one launch (start us, length us, event | category | flops | bytes accessed | tf_op | source)
XLA Modules:
  0.0 355.6 jit_solution(7723739133771676571)
XLA Ops:
  0.6 1.6 constant_dynamic-update-slice_fusion.47
  2.2 1.5 constant_dynamic-update-slice_fusion.46
  3.8 1.5 constant_dynamic-update-slice_fusion.45
  5.3 1.5 constant_dynamic-update-slice_fusion.44
  6.9 1.5 constant_dynamic-update-slice_fusion.43
  8.4 1.5 constant_dynamic-update-slice_fusion.42
  10.0 1.5 constant_dynamic-update-slice_fusion.41
  11.5 1.5 constant_dynamic-update-slice_fusion.40
  13.0 1.5 constant_dynamic-update-slice_fusion.39
  14.6 1.5 constant_dynamic-update-slice_fusion.38
  16.1 1.5 constant_dynamic-update-slice_fusion.37
  17.7 1.5 constant_dynamic-update-slice_fusion.36
  19.2 1.5 constant_dynamic-update-slice_fusion.35
  22.3 1.5 constant_dynamic-update-slice_fusion.33
  25.4 6.6 %all-to-all-start.4 = ((bf16[16,1,128,384]{3,2,1,0:T(8,128)(2,1)}), bf16[16,1,128,384]{3,2,1,0:T(8,128)(2,1)S(1)}, u32[]{:S(2)}, u32[]{:S(2)}) async-start(bf16[16,1,128,384]{3,2,1,0:T(8,128)(2,1)} %constant_dynamic-update-slice_fusion.32), calls=%async_computation.4 | async-start | bytes 3145728 | tf_op jit(solution)/shard_map/all_to_all | solution.py:50
  33.5 1.5 constant_dynamic-update-slice_fusion.30
  36.6 1.5 constant_dynamic-update-slice_fusion.28
  44.3 1.5 constant_dynamic-update-slice_fusion.23
  52.0 1.5 constant_dynamic-update-slice_fusion.18
  55.1 1.5 constant_dynamic-update-slice_fusion.16
  56.7 11.8 %all-to-all-done.4 = bf16[16,1,128,384]{3,2,1,0:T(8,128)(2,1)S(1)} async-done(((bf16[16,1,128,384]{3,2,1,0:T(8,128)(2,1)}), bf16[16,1,128,384]{3,2,1,0:T(8,128)(2,1)S(1)}, u32[]{:S(2)}, u32[]{:S(2)}) %all-to-all-start.4) | async-done | bytes 1572896 | tf_op jit(solution)/shard_map/all_to_all | solution.py:50
  68.4 4.6 %all-to-all-start.3 = ((bf16[16,1,128,384]{3,2,1,0:T(8,128)(2,1)}), bf16[16,1,128,384]{3,2,1,0:T(8,128)(2,1)}, u32[]{:S(2)}, u32[]{:S(2)}) async-start(bf16[16,1,128,384]{3,2,1,0:T(8,128)(2,1)} %constant_dynamic-update-slice_fusion.16), calls=%async_computation.3 | async-start | bytes 3145728 | tf_op jit(solution)/shard_map/all_to_all | solution.py:50
  73.5 2.2 convolution_convert_fusion
  75.7 33.6 %all-to-all-done.3 = bf16[16,1,128,384]{3,2,1,0:T(8,128)(2,1)} async-done(((bf16[16,1,128,384]{3,2,1,0:T(8,128)(2,1)}), bf16[16,1,128,384]{3,2,1,0:T(8,128)(2,1)}, u32[]{:S(2)}, u32[]{:S(2)}) %all-to-all-start.3) | async-done | bytes 1572896 | tf_op jit(solution)/shard_map/all_to_all | solution.py:50
  109.3 4.8 %all-to-all-start = ((bf16[16,72,1024]{2,1,0:T(8,128)(2,1)}), bf16[16,72,1024]{2,1,0:T(8,128)(2,1)}, u32[]{:S(2)}, u32[]{:S(2)}) async-start(bf16[16,72,1024]{2,1,0:T(8,128)(2,1)} %bitcast.2), calls=%async_computation | async-start | bytes 4718592 | tf_op jit(solution)/shard_map/all_to_all | solution.py:46
  114.6 2.2 fusion
  116.8 50.1 %all-to-all-done = bf16[16,72,1024]{2,1,0:T(8,128)(2,1)} async-done(((bf16[16,72,1024]{2,1,0:T(8,128)(2,1)}), bf16[16,72,1024]{2,1,0:T(8,128)(2,1)}, u32[]{:S(2)}, u32[]{:S(2)}) %all-to-all-start) | async-done | bytes 2359328 | tf_op jit(solution)/shard_map/all_to_all | solution.py:46
  167.0 4.6 %all-to-all-start.1 = ((bf16[16,72,1024]{2,1,0:T(8,128)(2,1)}), bf16[16,72,1024]{2,1,0:T(8,128)(2,1)}, u32[]{:S(2)}, u32[]{:S(2)}) async-start(bf16[16,72,1024]{2,1,0:T(8,128)(2,1)} %bitcast.5), calls=%async_computation.1 | async-start | bytes 4718592 | tf_op jit(solution)/shard_map/all_to_all | solution.py:46
  176.1 1.5 constant_dynamic-update-slice_fusion.12
  179.2 1.5 constant_dynamic-update-slice_fusion.10
  186.9 1.5 constant_dynamic-update-slice_fusion.5
  188.5 2.3 collective-permute-start
  190.8 1.5 constant_dynamic-update-slice_fusion.4
  198.5 25.9 %all-to-all-done.1 = bf16[16,72,1024]{2,1,0:T(8,128)(2,1)} async-done(((bf16[16,72,1024]{2,1,0:T(8,128)(2,1)}), bf16[16,72,1024]{2,1,0:T(8,128)(2,1)}, u32[]{:S(2)}, u32[]{:S(2)}) %all-to-all-start.1) | async-done | bytes 2359328 | tf_op jit(solution)/shard_map/all_to_all | solution.py:46
  224.5 4.6 %all-to-all-start.2 = ((bf16[16,1,128,384]{3,2,1,0:T(8,128)(2,1)}), bf16[16,1,128,384]{3,2,1,0:T(8,128)(2,1)}, u32[]{:S(2)}, u32[]{:S(2)}) async-start(bf16[16,1,128,384]{3,2,1,0:T(8,128)(2,1)} %constant_dynamic-update-slice_fusion), calls=%async_computation.2 | async-start | bytes 3145728 | tf_op jit(solution)/shard_map/all_to_all | solution.py:50
  229.0 2.3 collective-permute-start.1
  231.4 7.7 %fusion.29 = f32[1152,384]{1,0:T(8,128)} fusion(bf16[2048,384]{1,0:T(8,128)(2,1)S(1)} %bitcast.133, bf16[1152,1024]{1,0:T(8,128)(2,1)} %collective-permute-done, bf16[1152,1024]{1,0:T(8,128)(2,1)} %bitcast.3, pred[]{:T(512)S(6)} %eq.42), kind=kOutput, calls=%fused_computation.98 | convolution fusion | flops 1833172992 | bytes 8060929 | tf_op jit(solution)/shard_map/dot_general | solution.py:63
  239.0 8.0 %fusion.30 = f32[1152,384]{1,0:T(8,128)} fusion(bf16[2048,384]{1,0:T(8,128)(2,1)} %bitcast.40, bf16[1152,1024]{1,0:T(8,128)(2,1)} %collective-permute-done, bf16[1152,1024]{1,0:T(8,128)(2,1)} %bitcast.3, pred[]{:T(512)S(6)} %eq.42), kind=kOutput, calls=%fused_computation.99 | convolution fusion | flops 1833172992 | bytes 8060929 | tf_op jit(solution)/shard_map/dot_general | solution.py:64
  247.0 18.2 %all-to-all-done.2 = bf16[16,1,128,384]{3,2,1,0:T(8,128)(2,1)} async-done(((bf16[16,1,128,384]{3,2,1,0:T(8,128)(2,1)}), bf16[16,1,128,384]{3,2,1,0:T(8,128)(2,1)}, u32[]{:S(2)}, u32[]{:S(2)}) %all-to-all-start.2) | async-done | bytes 1572896 | tf_op jit(solution)/shard_map/all_to_all | solution.py:50
  265.3 7.4 %multiply_convert_fusion.1 = (bf16[1152,384]{1,0:T(8,128)(2,1)S(1)}, bf16[1152,384]{1,0:T(8,128)(2,1)S(1)}) fusion(f32[1152,384]{1,0:T(8,128)} %fusion.29, f32[1152,384]{1,0:T(8,128)} %fusion.30, bf16[2048,384]{1,0:T(8,128)(2,1)} %bitcast.23, bf16[1152,1024]{1,0:T(8,128)(2,1)} %collective-permute-done.1, bf16[1152,1024]{1,0:T(8,128)(2,1)} %bitcast.6, ...), kind=kOutput, calls=%fused_computation.16 | convolution fusion | flops 1838923776 | bytes 11599873 | tf_op jit(solution)/shard_map/dot_general | solution.py:67
  274.2 2.6 fusion.1
  279.4 2.7 collective-permute-done.2
  282.1 4.0 %add_convert_fusion = bf16[1152,1024]{1,0:T(8,128)(2,1)} fusion(bf16[1152,1024]{1,0:T(8,128)(2,1)S(1)} %collective-permute-done.2, f32[1152,1024]{1,0:T(8,128)S(1)} %fusion.14, bf16[1152,384]{1,0:T(8,128)(2,1)S(1)} %get-tuple-element.4, bf16[2048,384]{1,0:T(8,128)(2,1)} %bitcast.40, s32[]{:T(128)S(6)} %select_n.45), kind=kOutput, calls=%fused_computation.5 | convolution fusion | flops 910688256 | bytes 11108356 | tf_op jit(solution)/shard_map/dot_general | solution.py:76
  286.1 5.1 %all-to-all-start.5 = ((bf16[16,72,1024]{2,1,0:T(8,128)(2,1)}), bf16[16,72,1024]{2,1,0:T(8,128)(2,1)S(1)}, u32[]{:S(2)}, u32[]{:S(2)}) async-start(bf16[16,72,1024]{2,1,0:T(8,128)(2,1)} %bitcast.132), calls=%async_computation.5 | async-start | bytes 4718592 | tf_op jit(solution)/shard_map/all_to_all | solution.py:46
  291.2 8.1 %fusion.3 = bf16[1,2048,384]{2,1,0:T(8,128)(2,1)} fusion(bf16[1152,384]{1,0:T(8,128)(2,1)} %copy-done.3, bf16[1152,1024]{1,0:T(8,128)(2,1)} %collective-permute-done, bf16[1152,1024]{1,0:T(8,128)(2,1)} %bitcast.3, pred[]{:T(512)S(6)} %eq.42), kind=kOutput, calls=%fused_computation.13 | convolution fusion | flops 1833959424 | bytes 7176193 | tf_op jit(solution)/shard_map/dot_general | solution.py:88
  299.4 8.1 %fusion.4 = bf16[1,2048,384]{2,1,0:T(8,128)(2,1)} fusion(f32[1152,384]{1,0:T(8,128)S(1)} %copy-done.8, f32[1152,384]{1,0:T(8,128)S(1)} %copy-done.7, bf16[1152,1024]{1,0:T(8,128)(2,1)} %collective-permute-done.1, bf16[1152,1024]{1,0:T(8,128)(2,1)} %bitcast.6, pred[]{:T(512)S(6)} %eq.42), kind=kOutput, calls=%fused_computation.14 | convolution fusion | flops 1836613632 | bytes 9830401 | tf_op jit(solution)/shard_map/dot_general | solution.py:86
  307.5 37.3 %all-to-all-done.5 = bf16[16,72,1024]{2,1,0:T(8,128)(2,1)S(1)} async-done(((bf16[16,72,1024]{2,1,0:T(8,128)(2,1)}), bf16[16,72,1024]{2,1,0:T(8,128)(2,1)S(1)}, u32[]{:S(2)}, u32[]{:S(2)}) %all-to-all-start.5) | async-done | bytes 2359328 | tf_op jit(solution)/shard_map/all_to_all | solution.py:46
  346.8 7.8 %fusion.2 = bf16[1,2048,384]{2,1,0:T(8,128)(2,1)} fusion(bf16[1152,384]{1,0:T(8,128)(2,1)S(1)} %copy-done.2, bf16[1152,1024]{1,0:T(8,128)(2,1)} %collective-permute-done, bf16[1152,1024]{1,0:T(8,128)(2,1)} %bitcast.3, pred[]{:T(512)S(6)} %eq.42), kind=kOutput, calls=%fused_computation.12 | convolution fusion | flops 1833959424 | bytes 7176193 | tf_op jit(solution)/shard_map/dot_general | solution.py:87
  (60 shorter events, 46.5 us)
Async XLA Ops:
  0.6 72.9 %copy-start = (bf16[128,2048]{1,0:T(8,128)(2,1)S(1)}, bf16[128,2048]{1,0:T(8,128)(2,1)}, u32[]{:S(2)}) copy-start(bf16[128,2048]{1,0:T(8,128)(2,1)} %param.7) | copy-start | bytes 1572868
  25.4 43.1 %all-to-all-start.4 = ((bf16[16,1,128,384]{3,2,1,0:T(8,128)(2,1)}), bf16[16,1,128,384]{3,2,1,0:T(8,128)(2,1)S(1)}, u32[]{:S(2)}, u32[]{:S(2)}) async-start(bf16[16,1,128,384]{3,2,1,0:T(8,128)(2,1)} %constant_dynamic-update-slice_fusion.32), calls=%async_computation.4 | async-start | bytes 3145728 | tf_op jit(solution)/shard_map/all_to_all | solution.py:50
  56.6 16.4 %copy-start.5 = (s32[128,8]{0,1:T(8,128)S(1)}, s32[128,8]{0,1:T(8,128)}, u32[]{:S(2)}) copy-start(s32[128,8]{0,1:T(8,128)} %param.9) | copy-start | bytes 12292
  68.4 40.9 %all-to-all-start.3 = ((bf16[16,1,128,384]{3,2,1,0:T(8,128)(2,1)}), bf16[16,1,128,384]{3,2,1,0:T(8,128)(2,1)}, u32[]{:S(2)}, u32[]{:S(2)}) async-start(bf16[16,1,128,384]{3,2,1,0:T(8,128)(2,1)} %constant_dynamic-update-slice_fusion.16), calls=%async_computation.3 | async-start | bytes 3145728 | tf_op jit(solution)/shard_map/all_to_all | solution.py:50
  109.3 4.8 %copy-start.6 = (f32[128,8]{0,1:T(8,128)S(1)}, f32[128,8]{0,1:T(8,128)}, u32[]{:S(2)}) copy-start(f32[128,8]{0,1:T(8,128)} %param.10) | copy-start | bytes 12292
  109.3 5.2 %copy-start.4 = (bf16[128,2048]{1,0:T(8,128)(2,1)S(1)}, bf16[128,2048]{1,0:T(8,128)(2,1)}, u32[]{:S(2)}) copy-start(bf16[128,2048]{1,0:T(8,128)(2,1)} %param.8) | copy-start | bytes 1572868
  109.3 57.6 %all-to-all-start = ((bf16[16,72,1024]{2,1,0:T(8,128)(2,1)}), bf16[16,72,1024]{2,1,0:T(8,128)(2,1)}, u32[]{:S(2)}, u32[]{:S(2)}) async-start(bf16[16,72,1024]{2,1,0:T(8,128)(2,1)} %bitcast.2), calls=%async_computation | async-start | bytes 4718592 | tf_op jit(solution)/shard_map/all_to_all | solution.py:46
  167.0 57.5 %all-to-all-start.1 = ((bf16[16,72,1024]{2,1,0:T(8,128)(2,1)}), bf16[16,72,1024]{2,1,0:T(8,128)(2,1)}, u32[]{:S(2)}, u32[]{:S(2)}) async-start(bf16[16,72,1024]{2,1,0:T(8,128)(2,1)} %bitcast.5), calls=%async_computation.1 | async-start | bytes 4718592 | tf_op jit(solution)/shard_map/all_to_all | solution.py:46
  188.5 42.9 %collective-permute-start = (bf16[1152,1024]{1,0:T(8,128)(2,1)}, bf16[1152,1024]{1,0:T(8,128)(2,1)}, u32[]{:S(2)}, u32[]{:S(2)}) collective-permute-start(bf16[1152,1024]{1,0:T(8,128)(2,1)} %bitcast.3), channel_id=1, source_target_pairs={{0,16},{16,0},{1,17},{17,1},{2,18},{18,2},{3,19},{19,3},{4,20},{20... | collective-permute-start | bytes 7077896 | tf_op jit(solution)/shard_map/ppermute | solution.py:13
  224.5 40.8 %all-to-all-start.2 = ((bf16[16,1,128,384]{3,2,1,0:T(8,128)(2,1)}), bf16[16,1,128,384]{3,2,1,0:T(8,128)(2,1)}, u32[]{:S(2)}, u32[]{:S(2)}) async-start(bf16[16,1,128,384]{3,2,1,0:T(8,128)(2,1)} %constant_dynamic-update-slice_fusion), calls=%async_computation.2 | async-start | bytes 3145728 | tf_op jit(solution)/shard_map/all_to_all | solution.py:50
  229.0 36.3 %collective-permute-start.1 = (bf16[1152,1024]{1,0:T(8,128)(2,1)}, bf16[1152,1024]{1,0:T(8,128)(2,1)}, u32[]{:S(2)}, u32[]{:S(2)}) collective-permute-start(bf16[1152,1024]{1,0:T(8,128)(2,1)} %bitcast.6), channel_id=1, source_target_pairs={{0,16},{16,0},{1,17},{17,1},{2,18},{18,2},{3,19},{19,3},{4,20},{20... | collective-permute-start | bytes 7077896 | tf_op jit(solution)/shard_map/ppermute | solution.py:13
  272.7 5.2 %copy-start.1 = (bf16[1152,384]{1,0:T(8,128)(2,1)}, bf16[1152,384]{1,0:T(8,128)(2,1)S(1)}, u32[]{:S(2)}) copy-start(bf16[1152,384]{1,0:T(8,128)(2,1)S(1)} %get-tuple-element.5) | copy-start | bytes 2654212
  272.7 9.4 %copy-start.3 = (bf16[1152,384]{1,0:T(8,128)(2,1)}, bf16[1152,384]{1,0:T(8,128)(2,1)S(1)}, u32[]{:S(2)}) copy-start(bf16[1152,384]{1,0:T(8,128)(2,1)S(1)} %get-tuple-element.4) | copy-start | bytes 2654212
  276.8 5.3 %collective-permute-start.2 = (bf16[1152,1024]{1,0:T(8,128)(2,1)S(1)}, bf16[1152,1024]{1,0:T(8,128)(2,1)S(1)}, u32[]{:S(2)}, u32[]{:S(2)}) collective-permute-start(bf16[1152,1024]{1,0:T(8,128)(2,1)S(1)} %fusion.1), channel_id=1, source_target_pairs={{0,16},{16,0},{1,17},{17,1},{2,18},{18,2},{3,19},{19,3},{4,20},{20... | collective-permute-start | bytes 7077896 | tf_op jit(solution)/shard_map/ppermute | solution.py:13
  286.1 58.6 %all-to-all-start.5 = ((bf16[16,72,1024]{2,1,0:T(8,128)(2,1)}), bf16[16,72,1024]{2,1,0:T(8,128)(2,1)S(1)}, u32[]{:S(2)}, u32[]{:S(2)}) async-start(bf16[16,72,1024]{2,1,0:T(8,128)(2,1)} %bitcast.132), calls=%async_computation.5 | async-start | bytes 4718592 | tf_op jit(solution)/shard_map/all_to_all | solution.py:46
  291.2 8.2 %copy-start.7 = (f32[1152,384]{1,0:T(8,128)S(1)}, f32[1152,384]{1,0:T(8,128)}, u32[]{:S(2)}) copy-start(f32[1152,384]{1,0:T(8,128)} %fusion.29) | copy-start | bytes 5308420
  291.2 8.2 %copy-start.8 = (f32[1152,384]{1,0:T(8,128)S(1)}, f32[1152,384]{1,0:T(8,128)}, u32[]{:S(2)}) copy-start(f32[1152,384]{1,0:T(8,128)} %fusion.30) | copy-start | bytes 5308420
  344.8 2.0 copy-start.2
  345.4 9.3 %collective-permute-start.3 = (bf16[128,1024]{1,0:T(8,128)(2,1)S(1)}, bf16[128,1024]{1,0:T(8,128)(2,1)S(1)}, u32[]{:S(2)}, u32[]{:S(2)}) collective-permute-start(bf16[128,1024]{1,0:T(8,128)(2,1)S(1)} %fusion.5), channel_id=1, source_target_pairs={{0,16},{16,0},{1,17},{17,1},{2,18},{18,2},{3,19},{19,3},{4,20},{20... | collective-permute-start | bytes 786440 | tf_op jit(solution)/shard_map/ppermute | solution.py:13
